TPU v7x, 32 devices: a whole 2x2x4 slice. The times are simulated.
32 devices in a mesh: dp: 16 (over z, y, x), tensor: 2 (over core).
Axes of the slice: x: 2, y: 2, z: 4, core: 2. Of those that a mesh axis runs over, the one named last changes fastest.
Arguments:
- resid: bfloat16 [64, 32, 8192], P('dp'), may hold values from -6 to 6
- norm_gain: float32 [8192], replicated, may hold values from 0.1 to 1.9
- w_value: bfloat16 [8192, 768], P('dp', 'tensor'), may hold values from -0.0625 to 0.0625
- d_value: bfloat16 [64, 32, 768], P('dp', None, 'tensor'), may hold values from -6 to 6
- rewards: bfloat16 [64], P('dp'), may hold values from 0 to 1
- lengths: int32 [16, 4], P('dp'), may hold values from 1 to 32, 96 in all within a row
Outputs:
- value: bfloat16 [64, 32, 768], P('dp', None, 'tensor')
- w_grad: bfloat16 [8192, 768], P('dp', 'tensor')
Inputs may be any that keep to these rules, and one draw needn't show every extreme that they name: The 4 responses of each index of dp have lengths that sum to exactly 96.
All inputs are finite; a program needn't handle non-finite values.
Results may differ from a plain program's by a relative error of at most 0.0058.
Values may be sent and summed in bfloat16 or wider, within the bound.
A program may use at most 64 MiB of HBM per device.

v0:
```python
import jax
import jax.numpy as jnp
from jax import lax
from jax.sharding import PartitionSpec as P

GROUP = 16


def per_device(resid, norm_gain, w_value, d_value, rewards, lengths):
    per_dp, slot_count, model_width = resid.shape
    head_cols = w_value.shape[1]
    dp_index = lax.axis_index("dp")
    all_rolls = per_dp * lax.axis_size("dp")
    own_rewards = rewards.astype(jnp.float32)
    roll_ids = jnp.arange(all_rolls, dtype=jnp.int32)
    local_ids = jnp.arange(per_dp, dtype=jnp.int32)
    place_match = roll_ids[:, None] == (dp_index * per_dp + local_ids)[None, :]
    spread_out = jnp.sum(jnp.where(place_match, own_rewards[None, :], 0.0), axis=1)
    every_reward = lax.psum(spread_out, "dp")
    group_start = dp_index * per_dp // GROUP * GROUP
    reward_grid = lax.dynamic_slice_in_dim(every_reward, group_start, GROUP, 0)
    group_mean = jnp.mean(reward_grid)
    group_spread = jnp.sqrt(jnp.mean((reward_grid - group_mean) ** 2))
    own_adv = (own_rewards - group_mean) / jnp.maximum(group_spread, 0.25)
    own_len = lengths.reshape(per_dp)
    coef_roll = -own_adv / own_len.astype(jnp.float32)
    resid_flat = resid.reshape(per_dp * slot_count, model_width)
    dval_flat = d_value.reshape(per_dp * slot_count, head_cols)
    slot_index = jnp.arange(per_dp * slot_count, dtype=jnp.int32)
    slot_roll = slot_index // slot_count
    slot_position = slot_index % slot_count
    roll_match = slot_roll[:, None] == local_ids[None, :]
    slot_len = jnp.sum(jnp.where(roll_match, own_len[None, :], 0), axis=1)
    slot_live = (slot_position < slot_len).astype(jnp.float32)
    offsets = jnp.cumsum(own_len) - own_len
    live_total = per_dp * slot_count * 3 // 4
    packed_slot = jnp.arange(live_total, dtype=jnp.int32)
    rollout_of = jnp.sum((packed_slot[:, None] >= offsets[None, :]).astype(jnp.int32), axis=1) - 1
    pack_match = rollout_of[:, None] == local_ids[None, :]
    position = packed_slot - jnp.sum(jnp.where(pack_match, offsets[None, :], 0), axis=1)
    source = rollout_of * slot_count + position
    state_rows = jnp.take(resid_flat, source, axis=0)
    dval_rows = jnp.take(dval_flat, source, axis=0)
    row_coef = jnp.sum(jnp.where(pack_match, coef_roll[None, :], 0.0), axis=1)
    live_mask = jnp.ones((live_total,), jnp.float32)
    states = state_rows.astype(jnp.float32)
    mean_sq = jnp.mean(states * states, axis=-1, keepdims=True)
    normed = (states * lax.rsqrt(mean_sq + 1e-05) * norm_gain).astype(jnp.bfloat16)
    columns = normed
    value_sum = jnp.dot(
        columns,
        lax.all_gather(w_value, "dp", axis=0, tiled=True),
        preferred_element_type=jnp.float32,
    )
    value_rows = (value_sum * live_mask[:, None]).astype(jnp.bfloat16)
    dscaled = (dval_rows.astype(jnp.float32) * (row_coef * live_mask)[:, None]).astype(jnp.bfloat16)
    columns = normed
    full_grad = lax.dot_general(
        columns, dscaled, (((0,), (0,)), ((), ())), preferred_element_type=jnp.float32
    )
    grad_share = lax.psum_scatter(full_grad, "dp", scatter_dimension=0, tiled=True)
    slot_offset = jnp.sum(jnp.where(roll_match, offsets[None, :], 0), axis=1)
    packed_index = jnp.clip(slot_offset + slot_position, 0, value_rows.shape[0] - 1)
    picked = jnp.take(value_rows, packed_index, axis=0)
    value_slots = jnp.where(slot_live[:, None] > 0.5, picked, jnp.zeros_like(picked))
    value = value_slots.reshape(per_dp, slot_count, head_cols)
    return (value, grad_share.astype(jnp.bfloat16))


def solution(mesh):
    return jax.shard_map(
        per_device,
        mesh=mesh,
        in_specs=(
            P("dp", None, None),
            P(),
            P("dp", "tensor"),
            P("dp", None, "tensor"),
            P("dp"),
            P("dp", None),
        ),
        out_specs=(P("dp", None, "tensor"), P("dp", "tensor")),
        check_vma=False,
    )
```

profile of v0, /device:TPU:0, one launch (start us, length us, event | category | flops | bytes accessed | tf_op | source)
XLA Modules:
  0.0 322.8 jit_solution(7093866501529109960)
XLA Ops:
  7.2 0.0 copy-start
  7.2 0.0 all-gather.2.cloned.1.call-start
  7.2 0.7 all-gather.2.cloned.1.call-update
  7.9 0.0 reduce-scatter.2.cloned.1.call-start
  8.0 0.7 convert_element_type.40
  8.6 0.1 select_reduce_fusion.1
  8.7 44.2 %psum.7 = f32[64]{0:T(128)S(1)} all-reduce(f32[64]{0:T(128)S(1)} %select_reduce_fusion.1), channel_id=1, replica_groups=mesh['dp'=16,'tensor'=2] {'dp'}, use_global_device_ids=true, to_apply=%region_7.8 | all-reduce | flops 64 | bytes 512 | tf_op jit(solution)/shard_map/psum | solution.py:19
  52.9 0.7 dynamic-slice_reduce_fusion
  54.2 0.7 multiply_reduce_fusion
  55.6 0.8 reduce-window_clone.1
  56.4 0.7 subtract_bitcast_fusion
  57.1 0.1 convert_reduce_fusion
  57.2 0.1 select_reduce_fusion.2
  57.3 1.7 gather_fusion.2
  59.0 0.0 copy-done
  59.0 0.0 copy-start.3
  59.0 0.0 copy-start.4
  59.0 0.0 copy-start.2
  59.0 2.7 gather_fusion
  61.7 0.1 select_reduce_fusion
  61.8 2.1 fusion
  63.9 7.0 %fusion.3 = f32[8192,384]{1,0:T(8,128)} fusion(f32[96]{0:T(128)S(1)} %select_reduce_fusion, bf16[96,384]{1,0:T(8,128)(2,1)S(1)} %gather_fusion.2, pred[96]{0:T(512)(128)(4,1)S(1)} %compare_and_fusion, f32[8192]{0:T(1024)S(1)} %copy-done.2, f32[96]{0:T(128)S(1)} %add_rsqrt_fusion, bf16[96,8192]{1,0:T(8,128)(2,1)S(1)} %copy-done.1), kind=kOutput, calls=%fused_computation.12 | convolution fusion | flops 608059392 | bytes 14263136 | tf_op jit(solution)/shard_map/dot_general | solution.py:58
  70.9 0.0 reduce-scatter.2.cloned.1.call-update
  70.9 0.1 select_reduce_fusion.4
  71.0 0.1 reduce_sum.92
  71.1 0.1 reduce_sum.90
  71.2 35.8 %all-gather.2.cloned.1.call-done = bf16[8192,384]{1,0:T(8,128)(2,1)} async-done(((bf16[512,384]{1,0:T(8,128)(2,1)}), bf16[8192,384]{1,0:T(8,128)(2,1)}) %all-gather.2.cloned.1.call-update) | async-done | bytes 6291472 | tf_op jit(solution)/shard_map/all_gather | solution.py:52
  107.0 4.5 %convolution_convert_fusion = bf16[96,384]{1,0:T(8,128)(2,1)S(1)} fusion(bf16[8192,384]{1,0:T(8,128)(2,1)} %all-gather.2.cloned.1.call-done, f32[8192]{0:T(1024)S(1)} %copy-done.2, f32[96]{0:T(128)S(1)} %add_rsqrt_fusion, bf16[96,8192]{1,0:T(8,128)(2,1)} %gather_fusion, pred[96]{0:T(512)(128)(4,1)S(1)} %compare_and_fusion), kind=kOutput, calls=%fused_computation.9 | convolution fusion | flops 607948800 | bytes 7971296 | tf_op jit(solution)/shard_map/dot_general | solution.py:50
  111.5 0.9 gather_fusion.1
  112.4 0.8 select_select_fusion
  113.1 200.9 %reduce-scatter.2.cloned.1.call-done = f32[512,384]{1,0:T(8,128)} async-done(((f32[8192,384]{1,0:T(8,128)}), f32[512,384]{1,0:T(8,128)}) %reduce-scatter.2.cloned.1.call-update) | async-done | bytes 786448 | tf_op jit(solution)/shard_map/reduce_scatter | solution.py:61
  314.0 1.9 convert_element_type.43
  (16 shorter events, 0.1 us)
Async XLA Ops:
  7.2 51.8 %copy-start = (bf16[4,32,8192]{2,1,0:T(8,128)(2,1)S(1)}, bf16[4,32,8192]{2,1,0:T(8,128)(2,1)}, u32[]{:S(2)}) copy-start(bf16[4,32,8192]{2,1,0:T(8,128)(2,1)} %param.6) | copy-start | bytes 6291460
  7.2 99.9 %all-gather.2.cloned.1.call-start = ((), (), s32[]{:S(2)}) async-start(), calls=%async_computation.1 | async-start | bytes 6684672 | tf_op jit(solution)/shard_map/all_gather | solution.py:52
  7.9 306.1 %reduce-scatter.2.cloned.1.call-start = ((), (), s32[]{:S(2)}) async-start(), calls=%async_computation.2 | async-start | bytes 13369344 | tf_op jit(solution)/shard_map/reduce_scatter | solution.py:61
  59.0 2.7 copy-start.3
  59.0 2.7 copy-start.4
  59.0 4.9 %copy-start.2 = (f32[8192]{0:T(1024)S(1)}, f32[8192]{0:T(1024)}, u32[]{:S(2)}) copy-start(f32[8192]{0:T(1024)} %param.7) | copy-start | bytes 98308
  61.7 2.2 copy-start.1
Sparse Core Ops, SparseCore 0:
  10.8 96.2 all-gather.1
  112.7 201.2 reduce-scatter.1
where the time goes:
time: 323 us
  waiting for transfers between devices  237 us (73%)
  blocking collectives  44.2 us (14%)
  between operations  15.5 us (5%)
  matrix products  11.4 us (4%)
  other arithmetic  8.78 us (3%)
  local copies, waits for them, and re-layouts  5.43 us (2%)
    reduce_scatter x1, waiting for transfers between devices, per_device(): lax.psum_scatter(full_grad, 'dp', scatter_dimension=0, tiled=True)  201 us
    psum x1, blocking collectives, per_device(): every_reward = lax.psum(spread_out, 'dp')  44.2 us
    all_gather x1, waiting for transfers between devices, per_device(): lax.all_gather(w_value, 'dp', axis=0, tiled=True)  35.8 us
    dot_general x1, matrix products, per_device(): lax.dot_general(columns, dscaled, (((0,), (0,)), ((), ())), preferred_ele...  6.98 us
  transfers between devices with their start and end apart: 2, of which 2 were waited for; matrix products, arithmetic and copies ran while one was open for 7% of the time, Pallas kernels for 0%

commit v1 on v0

v1 whole, which is shorter than its diff:
```python
import functools

import jax
import jax.numpy as jnp
from jax import lax
from jax.experimental import pallas as pl
from jax.experimental.pallas import tpu as pltpu
from jax.sharding import PartitionSpec as P

GROUP = 16
MESH = pl.DeviceIdType.MESH
F32 = jnp.float32
BF16 = jnp.bfloat16


def each(low, high, body):
    if high - low <= 4:
        for i in range(low, high):
            body(i)
    else:
        lax.fori_loop(low, high, lambda i, c: (body(i), c)[1], 0)


def kernel(
    n, tensor, per_dp, slots, live,
    resid_ref, gain_ref, w_ref, dval_ref, rew_ref, len_ref,
    value_ref, grad_ref,
    rew_all, nbuf, nrecv, dall, pbuf, pacc, vone, vtwo_out, vtwo, gacc, wpad,
    r_send, r_recv, n_send, n_recv, f_send, f_recv,
    d_send, d_recv, g_send, a_send, a_recv, b_send, b_recv,
):
    plane = GROUP // per_dp
    layers = n // plane
    total, width = resid_ref.shape
    feats = w_ref.shape[0]
    block = nbuf.shape[2]
    sub = block // feats
    share = tensor if live % (16 * tensor) == 0 else 1
    part = live // share

    d = lax.axis_index("dp")
    t = lax.axis_index("tensor")
    z = d // plane
    p = d % plane

    def rows_of(core):
        if share == 1:
            return pl.ds(0, live)
        return pl.ds(pl.multiple_of(core * part, 16), part)

    barrier = pltpu.get_barrier_semaphore()

    def greet(k):
        pl.semaphore_signal(
            barrier, inc=1, device_id={"dp": (d + k) % n, "tensor": t}, device_id_type=MESH
        )

    each(1, n, greet)
    for s in range(1, tensor):
        pl.semaphore_signal(
            barrier, inc=1, device_id={"dp": d, "tensor": (t + s) % tensor}, device_id_type=MESH
        )

    rew_all[p] = jnp.zeros(rew_all.shape[1:], F32)
    rew_all[p, 0:1, 0:per_dp] = rew_ref[...].astype(F32)

    slot_lane = lax.broadcasted_iota(jnp.int32, (1, total), 1)
    roll_lane = slot_lane // slots
    place = slot_lane % slots
    len_lane = jnp.zeros((1, total), jnp.int32)
    off_lane = jnp.zeros((1, total), jnp.int32)
    offset = jnp.int32(0)
    for j in range(per_dp):
        len_lane = jnp.where(roll_lane == j, len_ref[0, j], len_lane)
        off_lane = jnp.where(roll_lane == j, offset, off_lane)
        offset = offset + len_ref[0, j]
    target = jnp.where(place < len_lane, off_lane + place, -1)
    packed_row = lax.broadcasted_iota(jnp.int32, (live, total), 0)
    pack = jnp.where(packed_row == target, 1.0, 0.0).astype(BF16)

    chunk = 512 if width % 512 == 0 else 128
    lanes_sum = jnp.zeros((total, 128), F32)
    for c in range(width // chunk):
        x = resid_ref[:, c * chunk:(c + 1) * chunk].astype(F32)
        x = x * x
        for k in range(chunk // 128):
            lanes_sum = lanes_sum + x[:, k * 128:(k + 1) * 128]
    mean_sq = jnp.sum(lanes_sum, axis=1, keepdims=True) / width
    inv = lax.rsqrt(mean_sq + 1e-05)

    if sub == 1:
        wpad[...] = w_ref[...]
    else:
        for k in range(sub):
            wpad[k * feats:(k + 1) * feats, :] = jnp.where(
                d % sub == k, w_ref[...].astype(F32), 0.0
            ).astype(BF16)

    pl.semaphore_wait(barrier, n - 1 + tensor - 1)

    def reward_copy(k, slot):
        return pltpu.make_async_remote_copy(
            src_ref=rew_all.at[slot], dst_ref=rew_all.at[slot],
            send_sem=r_send.at[k], recv_sem=r_recv.at[slot],
            device_id={"dp": z * plane + (p + k) % plane, "tensor": t}, device_id_type=MESH,
        )

    for k in range(1, plane):
        reward_copy(k, p).start()

    def norm_block(j):
        at = pl.ds(pl.multiple_of((j // sub) * block, 128), block)
        x = resid_ref[:, at].astype(F32)
        normed = (x * inv * gain_ref[:, at]).astype(BF16)
        return jnp.dot(pack, normed, preferred_element_type=F32).astype(BF16)

    def norm_copy(j, source):
        return pltpu.make_async_remote_copy(
            src_ref=nbuf.at[j, rows_of(t)], dst_ref=nrecv.at[source, rows_of(t)],
            send_sem=n_send.at[j], recv_sem=n_recv.at[source],
            device_id={"dp": j, "tensor": t}, device_id_type=MESH,
        )

    def dest(dz, k):
        return ((z + dz) % layers) * plane + (p + k) % plane

    def origin(dz, k):
        return ((z + layers - dz) % layers) * plane + (p + plane - k) % plane

    def fill(dz):
        for k in range(plane):
            j = dest(dz, k)
            nbuf[j] = norm_block(j)

    def send_group(dz):
        for k in range(plane):
            norm_copy(dest(dz, k), d).start()

    fill(layers - 1)
    send_group(layers - 1)

    for k in range(1, plane):
        reward_copy(k, (p + plane - k) % plane).wait_recv()
    lane3 = lax.broadcasted_iota(jnp.int32, rew_all.shape, 2)
    sub3 = lax.broadcasted_iota(jnp.int32, rew_all.shape, 1)
    real = (lane3 < per_dp) & (sub3 == 0)
    rewards = jnp.where(real, rew_all[...], 0.0)

    def total_of(x):
        return jnp.sum(jnp.sum(jnp.sum(x, axis=0), axis=0, keepdims=True), axis=1, keepdims=True)

    mean = total_of(rewards) / GROUP
    away = jnp.where(real, rewards - mean[None], 0.0)
    spread = jnp.sqrt(total_of(away * away) / GROUP)
    own = rew_all[p][0:1, :]
    adv = (own - mean) / jnp.maximum(spread, 0.25)
    lane1 = lax.broadcasted_iota(jnp.int32, (1, 128), 1)
    len_of = jnp.ones((1, 128), jnp.int32)
    for j in range(per_dp):
        len_of = jnp.where(lane1 == j, len_ref[0, j], len_of)
    coef = -adv / len_of.astype(F32)
    slot_row = lax.broadcasted_iota(jnp.int32, (total, 128), 0) // slots
    lane2 = lax.broadcasted_iota(jnp.int32, (total, 128), 1)
    coef_row = jnp.sum(jnp.where(slot_row == lane2, coef, 0.0), axis=1, keepdims=True)
    scaled = (dval_ref[...].astype(F32) * coef_row).astype(BF16)
    dall[d] = jnp.dot(pack, scaled, preferred_element_type=F32).astype(BF16)

    def far_copy(dz, source):
        return pltpu.make_async_remote_copy(
            src_ref=dall.at[source], dst_ref=dall.at[source],
            send_sem=d_send.at[dz], recv_sem=d_recv.at[source],
            device_id={"dp": dest(dz, 0), "tensor": t}, device_id_type=MESH,
        )

    def near_copy(k, source):
        return pltpu.make_async_remote_copy(
            src_ref=dall.at[source], dst_ref=dall.at[source],
            send_sem=g_send.at[k, source // plane], recv_sem=d_recv.at[source],
            device_id={"dp": dest(0, k), "tensor": t}, device_id_type=MESH,
        )

    def rest(i):
        fill(layers - 2 - i)
        send_group(layers - 2 - i)

    if layers > 2:
        fill(layers - 2)
        each(1, layers, lambda dz: far_copy(dz, d).start())
        for k in range(1, plane):
            near_copy(k, d).start()
        send_group(layers - 2)
        each(1, layers - 2, rest)

    for k in range(1, plane):
        j = dest(0, k)
        nbuf[j] = norm_block(j)
    nrecv[d] = norm_block(d)
    if layers <= 2:
        each(1, layers, lambda dz: far_copy(dz, d).start())
        for k in range(1, plane):
            near_copy(k, d).start()
    for k in range(1, plane):
        norm_copy(dest(0, k), d).start()

    def pass_on(i):
        source = origin(layers - i, 0)
        far_copy(1, source).wait_recv()
        for k in range(1, plane):
            near_copy(k, source).start()

    each(1, layers, pass_on)

    def swap_copy(s, source, core):
        return pltpu.make_async_remote_copy(
            src_ref=nrecv.at[source, rows_of(core)], dst_ref=nrecv.at[source, rows_of(core)],
            send_sem=f_send.at[s, source], recv_sem=f_recv.at[s, source],
            device_id={"dp": d, "tensor": (t + s) % tensor}, device_id_type=MESH,
        )

    def value_copy(k, layer, writer):
        return pltpu.make_async_remote_copy(
            src_ref=pbuf.at[layer * plane + (p + plane - k) % plane],
            dst_ref=vone.at[writer, layer],
            send_sem=a_send.at[k, layer], recv_sem=a_recv.at[writer, layer],
            device_id={"dp": z * plane + (p + plane - k) % plane, "tensor": t}, device_id_type=MESH,
        )

    def take_in(dz, first):
        for k in range(first, plane):
            source = origin(dz, k)
            norm_copy(source, source).wait_recv()
            if share > 1:
                for s in range(1, tensor):
                    swap_copy(s, source, t).start()

    def multiply(dz, first):
        layer = (z + layers - dz) % layers
        for k in list(range(1, plane)) + [0]:
            source = origin(dz, k)
            if k >= first and share > 1:
                for s in range(1, tensor):
                    swap_copy(s, source, (t + tensor - s) % tensor).wait_recv()
            product = jnp.dot(nrecv[source], wpad[...], preferred_element_type=F32)
            if k == 0:
                pacc[layer] = product
            else:
                pbuf[source] = product.astype(BF16)
        for k in range(1, plane):
            value_copy(k, layer, p).start()

    def stage(i):
        dz = layers - i
        take_in(dz, 0)
        multiply(dz, 0)

    each(1, layers, stage)
    take_in(0, 1)
    multiply(0, 1)

    def plane_sum(layer):
        result = pacc[layer]
        for k in range(1, plane):
            writer = (p + k) % plane
            value_copy(k, layer, writer).wait_recv()
            result = result + vone[writer, layer].astype(F32)
        return result

    def layer_copy(layer, writer):
        return pltpu.make_async_remote_copy(
            src_ref=vtwo_out.at[layer], dst_ref=vtwo.at[writer],
            send_sem=b_send.at[layer], recv_sem=b_recv.at[writer],
            device_id={"dp": layer * plane + p, "tensor": t}, device_id_type=MESH,
        )

    def along(i):
        layer = (z + i) % layers
        vtwo_out[layer] = plane_sum(layer).astype(BF16)

    def along_send(i):
        layer_copy((z + i) % layers, z).start()

    each(1, layers, along)
    pacc[z] = plane_sum(z)
    each(1, layers, along_send)

    for k in range(1, plane):
        near_copy(k, z * plane + (p + k) % plane).wait_recv()

    def far_wait(dz):
        for k in range(1, plane):
            near_copy(k, origin(dz, k)).wait_recv()

    each(1, layers, far_wait)

    def grad_group(layer):
        at = pl.ds(layer * plane, plane)
        a = nrecv[at].reshape(plane * live, block)
        b = dall[at].reshape(plane * live, dall.shape[2])
        part_sum = lax.dot_general(
            a, b, (((0,), (0,)), ((), ())), preferred_element_type=F32
        )
        if isinstance(layer, int) and layer == 0:
            gacc[...] = part_sum
        else:
            gacc[...] = gacc[...] + part_sum

    grad_group(0)
    each(1, layers, grad_group)
    if sub == 1:
        grad_ref[...] = gacc[...].astype(BF16)
    else:
        chosen = gacc[0:feats, :]
        for k in range(1, sub):
            chosen = jnp.where(d % sub == k, gacc[k * feats:(k + 1) * feats, :], chosen)
        grad_ref[...] = chosen.astype(BF16)

    def add_in(i):
        writer = (z + i) % layers
        layer_copy(writer, writer).wait_recv()
        pacc[z] = pacc[z] + vtwo[writer].astype(F32)

    each(1, layers, add_in)
    rows = pacc[z].astype(BF16)
    value_ref[...] = lax.dot_general(
        pack, rows, (((0,), (0,)), ((), ())), preferred_element_type=F32
    ).astype(BF16)

    for k in range(1, plane):
        reward_copy(k, p).wait_send()

    def left(dz):
        far_copy(dz, d).wait_send()
        for k in range(plane):
            norm_copy(dest(dz, k), d).wait_send()
        layer_copy((z + dz) % layers, z).wait_send()

    each(1, layers, left)
    for k in range(1, plane):
        norm_copy(dest(0, k), d).wait_send()

    def left_too(layer):
        for k in range(1, plane):
            near_copy(k, layer * plane + p).wait_send()
            value_copy(k, layer, p).wait_send()

    each(0, layers, left_too)
    if share > 1:
        def left_swap(dz):
            for k in range(plane):
                for s in range(1, tensor):
                    swap_copy(s, origin(dz, k), t).wait_send()

        each(1, layers, left_swap)
        for k in range(1, plane):
            for s in range(1, tensor):
                swap_copy(s, origin(0, k), t).wait_send()


def per_device(n, tensor, resid, norm_gain, w_value, d_value, rewards, lengths):
    per_dp, slots, width = resid.shape
    feats, cols = w_value.shape
    total = per_dp * slots
    live = total * 3 // 4
    plane = GROUP // per_dp
    layers = n // plane
    block = max(feats, 128)
    dma = pltpu.SemaphoreType.DMA
    vmem = pl.BlockSpec(memory_space=pltpu.VMEM)
    value, grad = pl.pallas_call(
        functools.partial(kernel, n, tensor, per_dp, slots, live),
        out_shape=(
            jax.ShapeDtypeStruct((total, cols), BF16),
            jax.ShapeDtypeStruct((feats, cols), BF16),
        ),
        in_specs=[vmem] * 5 + [pl.BlockSpec(memory_space=pltpu.SMEM)],
        out_specs=(vmem, vmem),
        scratch_shapes=[
            pltpu.VMEM((plane, 8, 128), F32),
            pltpu.VMEM((n, live, block), BF16),
            pltpu.VMEM((n, live, block), BF16),
            pltpu.VMEM((n, live, cols), BF16),
            pltpu.VMEM((n, live, cols), BF16),
            pltpu.VMEM((layers, live, cols), F32),
            pltpu.VMEM((plane, layers, live, cols), BF16),
            pltpu.VMEM((layers, live, cols), BF16),
            pltpu.VMEM((layers, live, cols), BF16),
            pltpu.VMEM((block, cols), F32),
            pltpu.VMEM((block, cols), BF16),
            dma((plane,)), dma((plane,)),
            dma((n,)), dma((n,)),
            dma((tensor, n)), dma((tensor, n)),
            dma((layers,)), dma((n,)),
            dma((plane, layers)),
            dma((plane, layers)), dma((plane, layers)),
            dma((layers,)), dma((layers,)),
        ],
        compiler_params=pltpu.CompilerParams(
            collective_id=0, has_side_effects=True, vmem_limit_bytes=56 * 1024 * 1024
        ),
    )(
        resid.reshape(total, width),
        norm_gain.reshape(1, width),
        w_value,
        d_value.reshape(total, cols),
        rewards.reshape(1, per_dp),
        lengths,
    )
    return value.reshape(per_dp, slots, cols), grad


def solution(mesh):
    n, tensor = mesh.shape["dp"], mesh.shape["tensor"]
    return jax.shard_map(
        functools.partial(per_device, n, tensor),
        mesh=mesh,
        in_specs=(
            P("dp", None, None),
            P(),
            P("dp", "tensor"),
            P("dp", None, "tensor"),
            P("dp"),
            P("dp", None),
        ),
        out_specs=(P("dp", None, "tensor"), P("dp", "tensor")),
        check_vma=False,
    )
```

time: 323 us -> 61.7 us (0.19)
  waiting for transfers between devices: 237 us -> 0 us
  Pallas kernels: 0 us -> 57.5 us
  blocking collectives: 44.2 us -> 0 us
  between operations: 15.5 us -> 0.64 us
  matrix products: 11.4 us -> 0 us
  other arithmetic: 8.78 us -> 0 us
    reduce_scatter x1 -> x0, waiting for transfers between devices: 201 us -> none  [per_device(): lax.psum_scatter(full_grad, 'dp', scatter_dimension=0, tiled=True)]
    pallas_call x0 -> x1, Pallas kernels: none -> 57.5 us  [per_device(): pl.pallas_call(functools.partial(kernel, n, tensor, per_dp, slots, live),...]
    psum x1 -> x0, blocking collectives: 44.2 us -> none  [per_device(): every_reward = lax.psum(spread_out, 'dp')]
    all_gather x1 -> x0, waiting for transfers between devices: 35.8 us -> none  [per_device(): lax.all_gather(w_value, 'dp', axis=0, tiled=True)]
    dot_general x2 -> x0, matrix products: 11.4 us -> none  [the longest x1 6.98 us: per_device(): lax.dot_general(columns, dscaled, (((0,), (0,)), ((), ())), preferred_ele...]
    gather x3 -> x0, local copies, waits for them, and re-layouts: 5.24 us -> none  [the longest x1 2.69 us: per_device(): state_rows = jnp.take(resid_flat, source, axis=0)]
    reduce_sum x8 -> x0, other arithmetic: 3.86 us -> none  [the longest x1 2.08 us: per_device(): mean_sq = jnp.mean(states * states, axis=-1, keepdims=True)]
    unnamed x10 -> x2, local copies, waits for them, and re-layouts: 0.03 us -> 3.32 us
  transfers between devices with their start and end apart: 2 -> 0, of which waited for: 2 -> 0; matrix products, arithmetic and copies ran while one was open for 7% -> 0% of each run, Pallas kernels for 0% -> 0%
where the time goes in v1:
time: 61.7 us; the launch traced here: 61.5 us
  Pallas kernels  57.5 us (93%)
  local copies, waits for them, and re-layouts  3.32 us (5%)
  between operations  0.64 us (1%)
    pallas_call x1, Pallas kernels, per_device(): pl.pallas_call(functools.partial(kernel, n, tensor, per_dp, slots, live),...  57.5 us
    unnamed x2, local copies, waits for them, and re-layouts  3.32 us

profile of v1, /device:TPU:0, one launch (start us, length us, event | category | flops | bytes accessed | tf_op | source)
XLA Modules:
  0.0 61.5 jit_solution(13067203026763475199)
XLA Ops:
  0.6 57.5 %shard_map.77 = (bf16[128,384]{1,0:T(8,128)(2,1)}, bf16[512,384]{1,0:T(8,128)(2,1)}) custom-call(bf16[128,8192]{1,0:T(8,128)(2,1)} %bitcast.5, f32[1,8192]{1,0:T(1,128)} %bitcast.8, bf16[512,384]{1,0:T(8,128)(2,1)} %w_ref.1, bf16[128,384]{1,0:T(8,128)(2,1)} %bitcast.6, bf16[1,4]{1,0:T(2,128)(2,1)} %bitcast.9, s32[1,4]{1,0:T(1,128)} %len_ref.1), custom_call_target="tpu_custom_call" | custom-call | tf_op jit(solution)/shard_map/pallas_call | solution.py:369
  58.2 1.5 %copy.10 = bf16[4,32,384]{2,1,0:T(8,128)(2,1)} copy(bf16[4,32,384]{2,1,0:T(8,128)(2,1)} %bitcast.7) | data formatting | bytes 196608
  59.7 1.8 %copy.11 = bf16[512,384]{1,0:T(8,128)(2,1)} copy(bf16[512,384]{1,0:T(8,128)(2,1)} %get-tuple-element.9) | data formatting | bytes 786432

commit v2 on v1

--- a/solution.py
+++ b/solution.py
@@ -23,11 +23,12 @@
 
 def kernel(
     n, tensor, per_dp, slots, live,
-    resid_ref, gain_ref, w_ref, dval_ref, rew_ref, len_ref,
+    resid_hbm, gain_hbm, w_hbm, dval_hbm, rew_ref, len_ref,
     value_ref, grad_ref,
-    rew_all, nbuf, nrecv, dall, pbuf, pacc, vone, vtwo_out, vtwo, gacc, wpad,
-    r_send, r_recv, n_send, n_recv, f_send, f_recv,
-    d_send, d_recv, g_send, a_send, a_recv, b_send, b_recv,
+    resid_ref, gain_ref, w_ref, dval_ref,
+    rew_all, nbuf, nrecv, dall, pbuf, pkeep, pacc, vdiag, vone, vtwo_out, vtwo, gacc, wpad,
+    in_sem, r_send, r_recv, n_send, n_recv, f_send, f_recv,
+    l_send, d_recv, g_send, h_send, c_send, c_recv, a_send, a_recv, b_send, b_recv,
 ):
     plane = GROUP // per_dp
     layers = n // plane
@@ -42,6 +43,16 @@
     t = lax.axis_index("tensor")
     z = d // plane
     p = d % plane
+    across, up = p % 2, p // 2
+    peer = [p, up * 2 + 1 - across, (1 - up) * 2 + across, 3 - p]
+    half = live // 2
+
+    loads = [
+        pltpu.make_async_copy(source, place, in_sem.at[k])
+        for k, (source, place) in enumerate(
+            ((resid_hbm, resid_ref), (gain_hbm, gain_ref), (w_hbm, w_ref), (dval_hbm, dval_ref))
+        )
+    ]
 
     def rows_of(core):
         if share == 1:
@@ -60,6 +71,9 @@
         pl.semaphore_signal(
             barrier, inc=1, device_id={"dp": d, "tensor": (t + s) % tensor}, device_id_type=MESH
         )
+
+    for load in loads:
+        load.start()
 
     rew_all[p] = jnp.zeros(rew_all.shape[1:], F32)
     rew_all[p, 0:1, 0:per_dp] = rew_ref[...].astype(F32)
@@ -78,6 +92,9 @@
     packed_row = lax.broadcasted_iota(jnp.int32, (live, total), 0)
     pack = jnp.where(packed_row == target, 1.0, 0.0).astype(BF16)
 
+    for load in loads:
+        load.wait()
+
     chunk = 512 if width % 512 == 0 else 128
     lanes_sum = jnp.zeros((total, 128), F32)
     for c in range(width // chunk):
@@ -102,7 +119,7 @@
         return pltpu.make_async_remote_copy(
             src_ref=rew_all.at[slot], dst_ref=rew_all.at[slot],
             send_sem=r_send.at[k], recv_sem=r_recv.at[slot],
-            device_id={"dp": z * plane + (p + k) % plane, "tensor": t}, device_id_type=MESH,
+            device_id={"dp": z * plane + peer[k], "tensor": t}, device_id_type=MESH,
         )
 
     for k in range(1, plane):
@@ -122,10 +139,10 @@
         )
 
     def dest(dz, k):
-        return ((z + dz) % layers) * plane + (p + k) % plane
+        return ((z + dz) % layers) * plane + peer[k]
 
     def origin(dz, k):
-        return ((z + layers - dz) % layers) * plane + (p + plane - k) % plane
+        return ((z + layers - dz) % layers) * plane + peer[k]
 
     def fill(dz):
         for k in range(plane):
@@ -140,7 +157,7 @@
     send_group(layers - 1)
 
     for k in range(1, plane):
-        reward_copy(k, (p + plane - k) % plane).wait_recv()
+        reward_copy(k, peer[k]).wait_recv()
     lane3 = lax.broadcasted_iota(jnp.int32, rew_all.shape, 2)
     sub3 = lax.broadcasted_iota(jnp.int32, rew_all.shape, 1)
     real = (lane3 < per_dp) & (sub3 == 0)
@@ -165,19 +182,38 @@
     scaled = (dval_ref[...].astype(F32) * coef_row).astype(BF16)
     dall[d] = jnp.dot(pack, scaled, preferred_element_type=F32).astype(BF16)
 
-    def far_copy(dz, source):
+    def line_copy(way, source):
         return pltpu.make_async_remote_copy(
             src_ref=dall.at[source], dst_ref=dall.at[source],
-            send_sem=d_send.at[dz], recv_sem=d_recv.at[source],
-            device_id={"dp": dest(dz, 0), "tensor": t}, device_id_type=MESH,
+            send_sem=l_send.at[way, source // plane], recv_sem=d_recv.at[source, 0],
+            device_id={"dp": ((z + (1, layers - 1)[way]) % layers) * plane + p, "tensor": t},
+            device_id_type=MESH,
         )
 
     def near_copy(k, source):
         return pltpu.make_async_remote_copy(
             src_ref=dall.at[source], dst_ref=dall.at[source],
-            send_sem=g_send.at[k, source // plane], recv_sem=d_recv.at[source],
+            send_sem=g_send.at[k, source // plane], recv_sem=d_recv.at[source, 0],
             device_id={"dp": dest(0, k), "tensor": t}, device_id_type=MESH,
         )
+
+    def half_copy(h, source):
+        rows = pl.ds(h * half, half)
+        return pltpu.make_async_remote_copy(
+            src_ref=dall.at[source, rows], dst_ref=dall.at[source, rows],
+            send_sem=h_send.at[h, source // plane], recv_sem=d_recv.at[source, h],
+            device_id={"dp": dest(0, 2 - h), "tensor": t}, device_id_type=MESH,
+        )
+
+    room = (z + 1 < layers, z > 0)
+
+    def send_own():
+        for way in range(2):
+            @pl.when(room[way])
+            def _():
+                line_copy(way, d).start()
+        near_copy(1, d).start()
+        near_copy(2, d).start()
 
     def rest(i):
         fill(layers - 2 - i)
@@ -185,9 +221,7 @@
 
     if layers > 2:
         fill(layers - 2)
-        each(1, layers, lambda dz: far_copy(dz, d).start())
-        for k in range(1, plane):
-            near_copy(k, d).start()
+        send_own()
         send_group(layers - 2)
         each(1, layers - 2, rest)
 
@@ -196,19 +230,31 @@
         nbuf[j] = norm_block(j)
     nrecv[d] = norm_block(d)
     if layers <= 2:
-        each(1, layers, lambda dz: far_copy(dz, d).start())
-        for k in range(1, plane):
-            near_copy(k, d).start()
+        send_own()
     for k in range(1, plane):
         norm_copy(dest(0, k), d).start()
 
-    def pass_on(i):
-        source = origin(layers - i, 0)
-        far_copy(1, source).wait_recv()
-        for k in range(1, plane):
-            near_copy(k, source).start()
-
-    each(1, layers, pass_on)
+    def relay(h):
+        for way in range(2):
+            layer = z - h if way == 0 else z + h
+
+            @pl.when((layer >= 0) & (layer < layers))
+            def _():
+                source = layer * plane + p
+                line_copy(way, source).wait_recv()
+
+                @pl.when(room[way])
+                def _():
+                    line_copy(way, source).start()
+
+                near_copy(1, source).start()
+                near_copy(2, source).start()
+
+    def corner(layer):
+        for h in range(2):
+            source = layer * plane + peer[1 + h]
+            near_copy(1 + h, source).wait_recv()
+            half_copy(h, source).start()
 
     def swap_copy(s, source, core):
         return pltpu.make_async_remote_copy(
@@ -217,12 +263,19 @@
             device_id={"dp": d, "tensor": (t + s) % tensor}, device_id_type=MESH,
         )
 
-    def value_copy(k, layer, writer):
-        return pltpu.make_async_remote_copy(
-            src_ref=pbuf.at[layer * plane + (p + plane - k) % plane],
-            dst_ref=vone.at[writer, layer],
-            send_sem=a_send.at[k, layer], recv_sem=a_recv.at[writer, layer],
-            device_id={"dp": z * plane + (p + plane - k) % plane, "tensor": t}, device_id_type=MESH,
+    def corner_value(h, layer):
+        return pltpu.make_async_remote_copy(
+            src_ref=pbuf.at[layer * plane + peer[3], pl.ds(h * half, half)],
+            dst_ref=vdiag.at[h, layer],
+            send_sem=c_send.at[h, layer], recv_sem=c_recv.at[h, layer],
+            device_id={"dp": dest(0, 1 + h), "tensor": t}, device_id_type=MESH,
+        )
+
+    def value_copy(k, layer):
+        return pltpu.make_async_remote_copy(
+            src_ref=pbuf.at[layer * plane + peer[k]], dst_ref=vone.at[k - 1, layer],
+            send_sem=a_send.at[k, layer], recv_sem=a_recv.at[k, layer],
+            device_id={"dp": dest(0, k), "tensor": t}, device_id_type=MESH,
         )
 
     def take_in(dz, first):
@@ -235,7 +288,7 @@
 
     def multiply(dz, first):
         layer = (z + layers - dz) % layers
-        for k in list(range(1, plane)) + [0]:
+        for k in (3, 2, 1, 0):
             source = origin(dz, k)
             if k >= first and share > 1:
                 for s in range(1, tensor):
@@ -245,24 +298,34 @@
                 pacc[layer] = product
             else:
                 pbuf[source] = product.astype(BF16)
-        for k in range(1, plane):
-            value_copy(k, layer, p).start()
+            if k == 1:
+                pkeep[1, layer] = product[half:, :]
+            if k == 2:
+                pkeep[0, layer] = product[:half, :]
+        for h in range(2):
+            corner_value(h, layer).start()
 
     def stage(i):
         dz = layers - i
-        take_in(dz, 0)
-        multiply(dz, 0)
-
-    each(1, layers, stage)
-    take_in(0, 1)
-    multiply(0, 1)
+        first = 1 if isinstance(dz, int) and dz == 0 else 0
+        take_in(dz, first)
+        multiply(dz, first)
+
+    def merge(i):
+        layer = (z + i) % layers
+        for h in range(2):
+            corner_value(h, layer).wait_recv()
+            pbuf[layer * plane + peer[2 - h], pl.ds(h * half, half)] = (
+                pkeep[h, layer] + vdiag[h, layer].astype(F32)
+            ).astype(BF16)
+        for k in (1, 2):
+            value_copy(k, layer).start()
 
     def plane_sum(layer):
         result = pacc[layer]
-        for k in range(1, plane):
-            writer = (p + k) % plane
-            value_copy(k, layer, writer).wait_recv()
-            result = result + vone[writer, layer].astype(F32)
+        for k in (1, 2):
+            value_copy(k, layer).wait_recv()
+            result = result + vone[k - 1, layer].astype(F32)
         return result
 
     def layer_copy(layer, writer):
@@ -275,22 +338,39 @@
     def along(i):
         layer = (z + i) % layers
         vtwo_out[layer] = plane_sum(layer).astype(BF16)
-
-    def along_send(i):
-        layer_copy((z + i) % layers, z).start()
-
-    each(1, layers, along)
+        layer_copy(layer, z).start()
+
+    if layers == 4:
+        stage(1)
+        relay(1)
+        relay(2)
+        stage(2)
+        merge(1)
+        relay(3)
+        corner(z)
+        stage(3)
+        merge(2)
+        along(1)
+        stage(4)
+        merge(3)
+        along(2)
+        merge(4)
+        each(1, layers, lambda i: corner((z + i) % layers))
+        along(3)
+    else:
+        each(1, layers, relay)
+        each(0, layers, corner)
+        each(1, layers, stage)
+        stage(layers)
+        each(1, layers + 1, merge)
+        each(1, layers, along)
     pacc[z] = plane_sum(z)
-    each(1, layers, along_send)
-
-    for k in range(1, plane):
-        near_copy(k, z * plane + (p + k) % plane).wait_recv()
-
-    def far_wait(dz):
-        for k in range(1, plane):
-            near_copy(k, origin(dz, k)).wait_recv()
-
-    each(1, layers, far_wait)
+
+    def corner_wait(layer):
+        for h in range(2):
+            half_copy(h, layer * plane + peer[3]).wait_recv()
+
+    each(0, layers, corner_wait)
 
     def grad_group(layer):
         at = pl.ds(layer * plane, plane)
@@ -329,7 +409,6 @@
         reward_copy(k, p).wait_send()
 
     def left(dz):
-        far_copy(dz, d).wait_send()
         for k in range(plane):
             norm_copy(dest(dz, k), d).wait_send()
         layer_copy((z + dz) % layers, z).wait_send()
@@ -339,9 +418,18 @@
         norm_copy(dest(0, k), d).wait_send()
 
     def left_too(layer):
-        for k in range(1, plane):
+        for k in (1, 2):
             near_copy(k, layer * plane + p).wait_send()
-            value_copy(k, layer, p).wait_send()
+            value_copy(k, layer).wait_send()
+        for h in range(2):
+            half_copy(h, layer * plane + peer[1 + h]).wait_send()
+            corner_value(h, layer).wait_send()
+        for way in range(2):
+            behind = (layer <= z) if way == 0 else (layer >= z)
+
+            @pl.when(behind & room[way])
+            def _():
+                line_copy(way, layer * plane + p).wait_send()
 
     each(0, layers, left_too)
     if share > 1:
@@ -372,26 +460,32 @@
             jax.ShapeDtypeStruct((total, cols), BF16),
             jax.ShapeDtypeStruct((feats, cols), BF16),
         ),
-        in_specs=[vmem] * 5 + [pl.BlockSpec(memory_space=pltpu.SMEM)],
+        in_specs=[pl.BlockSpec(memory_space=pltpu.HBM)] * 4 + [vmem] + [pl.BlockSpec(memory_space=pltpu.SMEM)],
         out_specs=(vmem, vmem),
         scratch_shapes=[
+            pltpu.VMEM((total, width), BF16),
+            pltpu.VMEM((1, width), F32),
+            pltpu.VMEM((feats, cols), BF16),
+            pltpu.VMEM((total, cols), BF16),
             pltpu.VMEM((plane, 8, 128), F32),
             pltpu.VMEM((n, live, block), BF16),
             pltpu.VMEM((n, live, block), BF16),
             pltpu.VMEM((n, live, cols), BF16),
             pltpu.VMEM((n, live, cols), BF16),
+            pltpu.VMEM((2, layers, live // 2, cols), F32),
             pltpu.VMEM((layers, live, cols), F32),
-            pltpu.VMEM((plane, layers, live, cols), BF16),
+            pltpu.VMEM((2, layers, live // 2, cols), BF16),
+            pltpu.VMEM((2, layers, live, cols), BF16),
             pltpu.VMEM((layers, live, cols), BF16),
             pltpu.VMEM((layers, live, cols), BF16),
             pltpu.VMEM((block, cols), F32),
             pltpu.VMEM((block, cols), BF16),
-            dma((plane,)), dma((plane,)),
+            dma((4,)), dma((plane,)), dma((plane,)),
             dma((n,)), dma((n,)),
             dma((tensor, n)), dma((tensor, n)),
-            dma((layers,)), dma((n,)),
-            dma((plane, layers)),
-            dma((plane, layers)), dma((plane, layers)),
+            dma((2, layers)), dma((n, 2)), dma((3, layers)), dma((2, layers)),
+            dma((2, layers)), dma((2, layers)),
+            dma((3, layers)), dma((3, layers)),
             dma((layers,)), dma((layers,)),
         ],
         compiler_params=pltpu.CompilerParams(

time: 61.7 us -> 55 us (0.89)
  Pallas kernels: 57.5 us -> 50.8 us
    pallas_call x1, Pallas kernels: 57.5 us -> 50.8 us  [per_device(): pl.pallas_call(functools.partial(kernel, n, tensor, per_dp, slots, live),...]
where the time goes in v2:
time: 55 us; the launch traced here: 54.7 us
  Pallas kernels  50.8 us (92%)
  local copies, waits for them, and re-layouts  3.32 us (6%)
  between operations  0.64 us (1%)
    pallas_call x1, Pallas kernels, per_device(): pl.pallas_call(functools.partial(kernel, n, tensor, per_dp, slots, live),...  50.8 us
    unnamed x2, local copies, waits for them, and re-layouts  3.32 us

profile of v2, /device:TPU:0, one launch (start us, length us, event | category | flops | bytes accessed | tf_op | source)
XLA Modules:
  0.0 54.7 jit_solution(14553155670604573630)
XLA Ops:
  0.6 50.8 %shard_map.77 = (bf16[128,384]{1,0:T(8,128)(2,1)}, bf16[512,384]{1,0:T(8,128)(2,1)}) custom-call(bf16[128,8192]{1,0:T(8,128)(2,1)} %bitcast.5, f32[1,8192]{1,0:T(1,128)} %bitcast.8, bf16[512,384]{1,0:T(8,128)(2,1)} %w_hbm.1, bf16[128,384]{1,0:T(8,128)(2,1)} %bitcast.6, bf16[1,4]{1,0:T(2,128)(2,1)} %bitcast.9, s32[1,4]{1,0:T(1,128)} %len_ref.1), custom_call_target="tpu_custom_call" | custom-call | tf_op jit(solution)/shard_map/pallas_call | solution.py:457
  51.4 1.5 %copy.10 = bf16[4,32,384]{2,1,0:T(8,128)(2,1)} copy(bf16[4,32,384]{2,1,0:T(8,128)(2,1)} %bitcast.7) | data formatting | bytes 196608
  52.9 1.8 %copy.11 = bf16[512,384]{1,0:T(8,128)(2,1)} copy(bf16[512,384]{1,0:T(8,128)(2,1)} %get-tuple-element.9) | data formatting | bytes 786432

commit v3 on v2

--- a/solution.py
+++ b/solution.py
@@ -153,7 +153,13 @@
         for k in range(plane):
             norm_copy(dest(dz, k), d).start()
 
+    for k in range(1, plane):
+        j = dest(0, k)
+        nbuf[j] = norm_block(j)
+    nrecv[d] = norm_block(d)
     fill(layers - 1)
+    for k in range(1, plane):
+        norm_copy(dest(0, k), d).start()
     send_group(layers - 1)
 
     for k in range(1, plane):
@@ -219,20 +225,10 @@
         fill(layers - 2 - i)
         send_group(layers - 2 - i)
 
-    if layers > 2:
-        fill(layers - 2)
-        send_own()
-        send_group(layers - 2)
-        each(1, layers - 2, rest)
-
-    for k in range(1, plane):
-        j = dest(0, k)
-        nbuf[j] = norm_block(j)
-    nrecv[d] = norm_block(d)
-    if layers <= 2:
-        send_own()
-    for k in range(1, plane):
-        norm_copy(dest(0, k), d).start()
+    fill(layers - 2)
+    send_own()
+    send_group(layers - 2)
+    each(1, layers - 2, rest)
 
     def relay(h):
         for way in range(2):
@@ -341,21 +337,21 @@
         layer_copy(layer, z).start()
 
     if layers == 4:
+        stage(4)
+        relay(1)
+        corner(z)
         stage(1)
-        relay(1)
+        merge(4)
         relay(2)
         stage(2)
         merge(1)
         relay(3)
-        corner(z)
         stage(3)
         merge(2)
         along(1)
-        stage(4)
+        each(1, layers, lambda i: corner((z + i) % layers))
         merge(3)
         along(2)
-        merge(4)
-        each(1, layers, lambda i: corner((z + i) % layers))
         along(3)
     else:
         each(1, layers, relay)

time: 55 us -> 52.5 us (0.955)
  Pallas kernels: 50.8 us -> 48.3 us
    pallas_call x1, Pallas kernels: 50.8 us -> 48.3 us  [per_device(): pl.pallas_call(functools.partial(kernel, n, tensor, per_dp, slots, live),...]
where the time goes in v3:
time: 52.5 us; the launch traced here: 52.3 us
  Pallas kernels  48.3 us (92%)
  local copies, waits for them, and re-layouts  3.32 us (6%)
  between operations  0.64 us (1%)
    pallas_call x1, Pallas kernels, per_device(): pl.pallas_call(functools.partial(kernel, n, tensor, per_dp, slots, live),...  48.3 us
    unnamed x2, local copies, waits for them, and re-layouts  3.32 us

profile of v3, /device:TPU:0, one launch (start us, length us, event | category | flops | bytes accessed | tf_op | source)
XLA Modules:
  0.0 52.3 jit_solution(663632819335439088)
XLA Ops:
  0.6 48.3 %shard_map.77 = (bf16[128,384]{1,0:T(8,128)(2,1)}, bf16[512,384]{1,0:T(8,128)(2,1)}) custom-call(bf16[128,8192]{1,0:T(8,128)(2,1)} %bitcast.5, f32[1,8192]{1,0:T(1,128)} %bitcast.8, bf16[512,384]{1,0:T(8,128)(2,1)} %w_hbm.1, bf16[128,384]{1,0:T(8,128)(2,1)} %bitcast.6, bf16[1,4]{1,0:T(2,128)(2,1)} %bitcast.9, s32[1,4]{1,0:T(1,128)} %len_ref.1), custom_call_target="tpu_custom_call" | custom-call | tf_op jit(solution)/shard_map/pallas_call | solution.py:453
  49.0 1.5 %copy.10 = bf16[4,32,384]{2,1,0:T(8,128)(2,1)} copy(bf16[4,32,384]{2,1,0:T(8,128)(2,1)} %bitcast.7) | data formatting | bytes 196608
  50.5 1.8 %copy.11 = bf16[512,384]{1,0:T(8,128)(2,1)} copy(bf16[512,384]{1,0:T(8,128)(2,1)} %get-tuple-element.9) | data formatting | bytes 786432
